TPU v7x, 32 devices: a whole 2x2x4 slice. The times are simulated.
32 devices in a mesh: dp: 4 (over y, x), depth: 4 (over z), grid: 2 (over core).
Axes of the slice: x: 2, y: 2, z: 4, core: 2. Of those that a mesh axis runs over, the one named last changes fastest.
Arguments:
- tokens: bfloat16 [1024, 12288], P(('dp', 'depth'), 'grid'), may hold values from -6 to 6
- weight: bfloat16 [12288, 24576], P('grid', 'depth'), may hold values from -0.0546875 to 0.0546875
- cotangent: bfloat16 [1024, 24576], P(('dp', 'grid'), 'depth'), may hold values from -0.5 to 0.5
Outputs:
- hidden: bfloat16 [1024, 24576], P(('dp', 'grid'), 'depth')
- weight_grad: bfloat16 [12288, 24576], P(('grid', 'dp'), 'depth')
All inputs are finite; a program needn't handle non-finite values.
Results may differ from a plain program's by a relative error of at most 0.011.
Values may be sent and summed in bfloat16 or wider, within the bound.
No kernel may reach another device: no remote copies, remote signals or barrier semaphores. Data moves between devices by JAX's collectives and lax.ppermute only.
A program may use at most 192 MiB of HBM per device.

v0:
```python
import jax
import jax.numpy as jnp
from jax import lax
from jax.sharding import PartitionSpec as P


def gelu_tanh(values):
    return jax.nn.gelu(values, approximate=True)


def transposed_product(left, right):
    return lax.dot_general(
        left, right, (((0,), (0,)), ((), ())), preferred_element_type=jnp.float32
    )


def local(tokens, weight, cotangent):
    all_rows = lax.all_gather(tokens, ("dp", "depth"), axis=0, tiled=True)
    group_size = all_rows.shape[0] // lax.axis_size("dp")
    own_rows = lax.dynamic_slice_in_dim(all_rows, lax.axis_index("dp") * group_size, group_size, 0)
    partial_pre = jnp.dot(own_rows, weight, preferred_element_type=jnp.float32)
    preact = lax.psum_scatter(partial_pre, "grid", scatter_dimension=0, tiled=True)
    activated, pullback = jax.vjp(gelu_tanh, preact)
    hidden = activated.astype(jnp.bfloat16)
    grad_pre = pullback(cotangent.astype(jnp.float32))[0].astype(jnp.bfloat16)
    sub_width = all_rows.shape[1] // lax.axis_size("dp")
    columns = lax.dynamic_slice_in_dim(all_rows, lax.axis_index("dp") * sub_width, sub_width, 1)
    weight_grad = transposed_product(
        columns, lax.all_gather(grad_pre, ("dp", "grid"), axis=0, tiled=True)
    )
    return (hidden, weight_grad.astype(jnp.bfloat16))


def solution(mesh):
    return jax.shard_map(
        local,
        mesh=mesh,
        in_specs=(P(("dp", "depth"), "grid"), P("grid", "depth"), P(("dp", "grid"), "depth")),
        out_specs=(P(("dp", "grid"), "depth"), P(("grid", "dp"), "depth")),
        check_vma=False,
    )
```

profile of v0, /device:TPU:0, one launch (start us, length us, event | category | flops | bytes accessed | tf_op | source)
XLA Modules:
  0.0 322.6 jit_solution(14169711380635420403)
XLA Ops:
  7.2 0.0 all-gather.3.cloned.1.call-start
  7.2 0.7 all-gather.3.cloned.1.call-update
  7.9 0.0 reduce-scatter.2.cloned.1.call-start
  7.9 157.1 %all-gather.3.cloned.1.call-done = bf16[1024,6144]{1,0:T(8,128)(2,1)} async-done(((bf16[64,6144]{1,0:T(8,128)(2,1)}), bf16[1024,6144]{1,0:T(8,128)(2,1)}) %all-gather.3.cloned.1.call-update) | async-done | bytes 12582928 | tf_op jit(solution)/shard_map/all_gather | solution.py:18
  165.0 31.6 %fusion.11 = f32[256,6144]{1,0:T(8,128)} fusion(bf16[6144,6144]{1,0:T(8,128)(2,1)} %param.4, bf16[1024,6144]{1,0:T(8,128)(2,1)} %all-gather.3.cloned.1.call-done, s32[]{:T(128)S(6)} %select_n.6), kind=kOutput, calls=%fused_computation.17 | convolution fusion | flops 19327352832 | bytes 84934656 | tf_op jit(solution)/shard_map/dot_general | solution.py:21
  196.6 0.0 copy-start
  196.6 0.0 reduce-scatter.2.cloned.1.call-update
  196.6 0.0 all-gather.5.cloned.1.call-start
  196.7 12.3 %reduce-scatter.2.cloned.1.call-done = f32[128,6144]{1,0:T(8,128)} async-done(((f32[256,6144]{1,0:T(8,128)}), f32[128,6144]{1,0:T(8,128)}) %reduce-scatter.2.cloned.1.call-update) | async-done | bytes 3145744 | tf_op jit(solution)/shard_map/reduce_scatter | solution.py:22
  209.0 0.0 copy-done
  209.0 4.9 %fusion.2 = (bf16[128,6144]{1,0:T(8,128)(2,1)}, bf16[128,6144]{1,0:T(8,128)(2,1)}) fusion(bf16[128,6144]{1,0:T(8,128)(2,1)S(1)} %copy-done, f32[128,6144]{1,0:T(8,128)} %reduce-scatter.2.cloned.1.call-done), kind=kLoop, calls=%fused_computation.7 | loop fusion | flops 18087936 | bytes 7864320 | tf_op jit(solution)/shard_map/convert_element_type | solution.py:25
  213.9 0.0 all-gather.5.cloned.1.call-update
  214.0 74.2 %all-gather.5.cloned.1.call-done = bf16[1024,6144]{1,0:T(8,128)(2,1)} async-done(((bf16[128,6144]{1,0:T(8,128)(2,1)}), bf16[1024,6144]{1,0:T(8,128)(2,1)}) %all-gather.5.cloned.1.call-update) | async-done | bytes 12582928 | tf_op jit(solution)/shard_map/all_gather | solution.py:29
  288.1 27.9 %convolution_convert_fusion = bf16[1536,6144]{1,0:T(8,128)(2,1)} fusion(bf16[1024,6144]{1,0:T(8,128)(2,1)} %all-gather.5.cloned.1.call-done, bf16[1024,6144]{1,0:T(8,128)(2,1)} %all-gather.3.cloned.1.call-done, s32[]{:T(128)S(6)} %select_n.7), kind=kOutput, calls=%fused_computation | convolution fusion | flops 19336790016 | bytes 34603012 | tf_op jit(solution)/shard_map/dot_general | solution.py:12
Async XLA Ops:
  7.2 157.8 %all-gather.3.cloned.1.call-start = ((), (), s32[]{:S(2)}) async-start(), calls=%async_computation.1 | async-start | bytes 13369344 | tf_op jit(solution)/shard_map/all_gather | solution.py:18
  7.9 201.1 %reduce-scatter.2.cloned.1.call-start = ((), (), s32[]{:S(2)}) async-start(), calls=%async_computation.2 | async-start | bytes 9437184 | tf_op jit(solution)/shard_map/reduce_scatter | solution.py:22
  196.6 12.4 %copy-start = (bf16[128,6144]{1,0:T(8,128)(2,1)S(1)}, bf16[128,6144]{1,0:T(8,128)(2,1)}, u32[]{:S(2)}) copy-start(bf16[128,6144]{1,0:T(8,128)(2,1)} %param.5) | copy-start | bytes 4718596
  196.6 91.5 %all-gather.5.cloned.1.call-start = ((), (), s32[]{:S(2)}) async-start(), calls=%async_computation.3 | async-start | bytes 14155776 | tf_op jit(solution)/shard_map/all_gather | solution.py:29
Sparse Core Ops, SparseCore 0:
  10.8 154.1 all-gather.2
  196.8 12.2 reduce-scatter.1
  214.1 73.9 all-gather.4
where the time goes:
time: 323 us
  waiting for transfers between devices  244 us (76%)
  matrix products  59.5 us (18%)
  between operations  13.8 us (4%)
  other arithmetic  4.9 us (2%)
    all_gather x1, waiting for transfers between devices, local(): all_rows = lax.all_gather(tokens, ('dp', 'depth'), axis=0, tiled=True)  157 us
    all_gather x1, waiting for transfers between devices, local(): lax.all_gather(grad_pre, ('dp', 'grid'), axis=0, tiled=True)  74.2 us
    dot_general x1, matrix products, local(): partial_pre = jnp.dot(own_rows, weight, preferred_element_type=jnp.float32)  31.6 us
    dot_general x1, matrix products, transposed_product(): lax.dot_general(left, right, (((0,), (0,)), ((), ())), preferred_element_...  27.9 us
    reduce_scatter x1, waiting for transfers between devices, local(): lax.psum_scatter(partial_pre, 'grid', scatter_dimension=0, tiled=True)  12.3 us
  transfers between devices with their start and end apart: 3, of which 3 were waited for; matrix products, arithmetic and copies ran while one was open for 0% of the time, Pallas kernels for 0%

commit v1 on v0

--- a/solution.py
+++ b/solution.py
@@ -15,7 +15,15 @@
 
 
 def local(tokens, weight, cotangent):
-    all_rows = lax.all_gather(tokens, ("dp", "depth"), axis=0, tiled=True)
+    ways, here = (lax.axis_size(("dp", "depth")), lax.axis_index(("dp", "depth")))
+    grown, reach = (tokens, 1)
+    while reach < ways:
+        theirs = lax.ppermute(grown, ("dp", "depth"), [(d, d ^ reach) for d in range(ways)])
+        mine_first = jnp.concatenate([grown, theirs], axis=0)
+        theirs_first = jnp.concatenate([theirs, grown], axis=0)
+        grown = jnp.where(here & reach == 0, mine_first, theirs_first)
+        reach = 2 * reach
+    all_rows = grown
     group_size = all_rows.shape[0] // lax.axis_size("dp")
     own_rows = lax.dynamic_slice_in_dim(all_rows, lax.axis_index("dp") * group_size, group_size, 0)
     partial_pre = jnp.dot(own_rows, weight, preferred_element_type=jnp.float32)

time: 323 us -> 495 us (1.53)
  waiting for transfers between devices: 244 us -> 379 us
  other arithmetic: 4.9 us -> 33.5 us
  starting transfers between devices: 0.12 us -> 8.93 us
    ppermute x0 -> x4, waiting for transfers between devices: none -> 288 us  [local(): lax.ppermute(grown, ('dp', 'depth'), [(d, d ^ reach) for d in range(ways)])]
    all_gather x1 -> x0, waiting for transfers between devices: 157 us -> none  [local(): all_rows = lax.all_gather(tokens, ('dp', 'depth'), axis=0, tiled=True)]
    select_n x0 -> x4, other arithmetic: none -> 28.6 us  [local(): grown = jnp.where(here & reach == 0, mine_first, theirs_first)]
    ppermute x0 -> x4, starting transfers between devices: none -> 8.67 us  [local(): lax.ppermute(grown, ('dp', 'depth'), [(d, d ^ reach) for d in range(ways)])]
  transfers between devices with their start and end apart: 3 -> 6, of which waited for: 3 -> 6; matrix products, arithmetic and copies ran while one was open for 0% -> 0% of each run, Pallas kernels for 0% -> 0%
where the time goes in v1:
time: 495 us
  waiting for transfers between devices  379 us (77%)
  matrix products  59.5 us (12%)
  other arithmetic  33.5 us (7%)
  between operations  14.1 us (3%)
  starting transfers between devices  8.93 us (2%)
    ppermute x4, waiting for transfers between devices, local(): lax.ppermute(grown, ('dp', 'depth'), [(d, d ^ reach) for d in range(ways)])  288 us
    all_gather x1, waiting for transfers between devices, local(): lax.all_gather(grad_pre, ('dp', 'grid'), axis=0, tiled=True)  74.2 us
    dot_general x1, matrix products, local(): partial_pre = jnp.dot(own_rows, weight, preferred_element_type=jnp.float32)  31.6 us
    select_n x4, other arithmetic, local(): grown = jnp.where(here & reach == 0, mine_first, theirs_first)  28.6 us
    dot_general x1, matrix products, transposed_product(): lax.dot_general(left, right, (((0,), (0,)), ((), ())), preferred_element_...  27.9 us
    reduce_scatter x1, waiting for transfers between devices, local(): lax.psum_scatter(partial_pre, 'grid', scatter_dimension=0, tiled=True)  16.8 us
  transfers between devices with their start and end apart: 6, of which 6 were waited for; matrix products, arithmetic and copies ran while one was open for 0% of the time, Pallas kernels for 0%

profile of v1, /device:TPU:0, one launch (start us, length us, event | category | flops | bytes accessed | tf_op | source)
XLA Modules:
  0.0 494.9 jit_solution(11295684810354950888)
XLA Ops:
  7.2 0.0 reduce-scatter.2.cloned.1.call-start
  7.2 3.1 collective-permute-start
  10.3 17.8 %collective-permute-done = bf16[64,6144]{1,0:T(8,128)(2,1)S(1)} collective-permute-done((bf16[64,6144]{1,0:T(8,128)(2,1)}, bf16[64,6144]{1,0:T(8,128)(2,1)S(1)}, u32[]{:S(2)}, u32[]{:S(2)}) %collective-permute-start) | collective-permute-done | bytes 786464 | tf_op jit(solution)/shard_map/ppermute | solution.py:21
  28.1 1.7 maximum_select_fusion.3
  29.8 0.0 copy-start
  29.8 2.8 collective-permute-start.1
  32.7 0.0 copy-done
  32.7 67.5 %collective-permute-done.1 = bf16[128,6144]{1,0:T(8,128)(2,1)} collective-permute-done((bf16[128,6144]{1,0:T(8,128)(2,1)S(1)}, bf16[128,6144]{1,0:T(8,128)(2,1)}, u32[]{:S(2)}, u32[]{:S(2)}) %collective-permute-start.1) | collective-permute-done | bytes 1572896 | tf_op jit(solution)/shard_map/ppermute | solution.py:21
  100.2 3.4 maximum_select_fusion.2
  103.6 1.4 collective-permute-start.2
  105.1 67.9 %collective-permute-done.2 = bf16[256,6144]{1,0:T(8,128)(2,1)} collective-permute-done((bf16[256,6144]{1,0:T(8,128)(2,1)S(1)}, bf16[256,6144]{1,0:T(8,128)(2,1)}, u32[]{:S(2)}, u32[]{:S(2)}) %collective-permute-start.2) | collective-permute-done | bytes 3145760 | tf_op jit(solution)/shard_map/ppermute | solution.py:21
  172.9 7.7 %maximum_select_fusion.1 = bf16[512,6144]{1,0:T(8,128)(2,1)} fusion(bf16[256,6144]{1,0:T(8,128)(2,1)} %collective-permute-done.2, bf16[256,6144]{1,0:T(8,128)(2,1)S(1)} %maximum_select_fusion.2, pred[]{:T(512)S(6)} %eq.13), kind=kLoop, calls=%fused_computation.2 | loop fusion | flops 28311552 | bytes 12582913 | tf_op jit(solution)/shard_map/jit(_where)/select_n | solution.py:24
  180.6 1.3 collective-permute-start.3
  181.9 134.7 %collective-permute-done.3 = bf16[512,6144]{1,0:T(8,128)(2,1)} collective-permute-done((bf16[512,6144]{1,0:T(8,128)(2,1)}, bf16[512,6144]{1,0:T(8,128)(2,1)}, u32[]{:S(2)}, u32[]{:S(2)}) %collective-permute-start.3) | collective-permute-done | bytes 6291488 | tf_op jit(solution)/shard_map/ppermute | solution.py:21
  316.6 15.8 %maximum_select_fusion = bf16[1024,6144]{1,0:T(8,128)(2,1)} fusion(bf16[512,6144]{1,0:T(8,128)(2,1)} %collective-permute-done.3, bf16[512,6144]{1,0:T(8,128)(2,1)} %maximum_select_fusion.1, pred[]{:T(512)S(6)} %eq.12), kind=kLoop, calls=%fused_computation.1 | loop fusion | flops 56623104 | bytes 25165824 | tf_op jit(solution)/shard_map/jit(_where)/select_n | solution.py:24
  332.3 31.6 %fusion.11 = f32[256,6144]{1,0:T(8,128)} fusion(bf16[6144,6144]{1,0:T(8,128)(2,1)} %param.4, bf16[1024,6144]{1,0:T(8,128)(2,1)} %maximum_select_fusion, s32[]{:T(128)S(6)} %select_n.46), kind=kOutput, calls=%fused_computation.20 | convolution fusion | flops 19327352832 | bytes 84934656 | tf_op jit(solution)/shard_map/dot_general | solution.py:29
  363.9 0.0 copy-start.1
  364.0 0.0 reduce-scatter.2.cloned.1.call-update
  364.0 0.2 all-gather.2.cloned.1.call-start
  364.2 16.8 %reduce-scatter.2.cloned.1.call-done = f32[128,6144]{1,0:T(8,128)} async-done(((f32[256,6144]{1,0:T(8,128)}), f32[128,6144]{1,0:T(8,128)}) %reduce-scatter.2.cloned.1.call-update) | async-done | bytes 3145744 | tf_op jit(solution)/shard_map/reduce_scatter | solution.py:30
  381.0 0.0 copy-done.1
  381.0 4.9 fusion.2
  385.9 0.0 all-gather.2.cloned.1.call-update
  385.9 74.2 %all-gather.2.cloned.1.call-done = bf16[1024,6144]{1,0:T(8,128)(2,1)} async-done(((bf16[128,6144]{1,0:T(8,128)(2,1)}), bf16[1024,6144]{1,0:T(8,128)(2,1)}) %all-gather.2.cloned.1.call-update) | async-done | bytes 12582928 | tf_op jit(solution)/shard_map/all_gather | solution.py:37
  460.1 27.9 %convolution_convert_fusion = bf16[1536,6144]{1,0:T(8,128)(2,1)} fusion(bf16[1024,6144]{1,0:T(8,128)(2,1)} %all-gather.2.cloned.1.call-done, bf16[1024,6144]{1,0:T(8,128)(2,1)} %maximum_select_fusion, s32[]{:T(128)S(6)} %select_n.47), kind=kOutput, calls=%fused_computation | convolution fusion | flops 19336790016 | bytes 34603012 | tf_op jit(solution)/shard_map/dot_general | solution.py:12
Async XLA Ops:
  7.2 373.8 %reduce-scatter.2.cloned.1.call-start = ((), (), s32[]{:S(2)}) async-start(), calls=%async_computation.1 | async-start | bytes 9437184 | tf_op jit(solution)/shard_map/reduce_scatter | solution.py:30
  7.2 20.9 %collective-permute-start = (bf16[64,6144]{1,0:T(8,128)(2,1)}, bf16[64,6144]{1,0:T(8,128)(2,1)S(1)}, u32[]{:S(2)}, u32[]{:S(2)}) collective-permute-start(bf16[64,6144]{1,0:T(8,128)(2,1)} %param.3), channel_id=1, source_target_pairs={{0,2},{2,0},{4,6},{6,4},{8,10},{10,8},{12,14},{14,12},{16,18},{18,... | collective-permute-start | bytes 2359304 | tf_op jit(solution)/shard_map/ppermute | solution.py:21
  29.8 2.8 copy-start
  29.8 70.3 %collective-permute-start.1 = (bf16[128,6144]{1,0:T(8,128)(2,1)S(1)}, bf16[128,6144]{1,0:T(8,128)(2,1)}, u32[]{:S(2)}, u32[]{:S(2)}) collective-permute-start(bf16[128,6144]{1,0:T(8,128)(2,1)S(1)} %maximum_select_fusion.3), channel_id=1, source_target_pairs={{0,4},{2,6},{4,0},{6,2},{8,12},{10,14},{12,8},{14,10},{16,20},{18,... | collective-permute-start | bytes 4718600 | tf_op jit(solution)/shard_map/ppermute | solution.py:21
  103.6 69.3 %collective-permute-start.2 = (bf16[256,6144]{1,0:T(8,128)(2,1)S(1)}, bf16[256,6144]{1,0:T(8,128)(2,1)}, u32[]{:S(2)}, u32[]{:S(2)}) collective-permute-start(bf16[256,6144]{1,0:T(8,128)(2,1)S(1)} %maximum_select_fusion.2), channel_id=1, source_target_pairs={{0,8},{2,10},{4,12},{6,14},{8,0},{10,2},{12,4},{14,6},{16,24},{18,... | collective-permute-start | bytes 9437192 | tf_op jit(solution)/shard_map/ppermute | solution.py:21
  180.6 136.0 %collective-permute-start.3 = (bf16[512,6144]{1,0:T(8,128)(2,1)}, bf16[512,6144]{1,0:T(8,128)(2,1)}, u32[]{:S(2)}, u32[]{:S(2)}) collective-permute-start(bf16[512,6144]{1,0:T(8,128)(2,1)} %maximum_select_fusion.1), channel_id=1, source_target_pairs={{0,16},{2,18},{4,20},{6,22},{8,24},{10,26},{12,28},{14,30},{16,0},... | collective-permute-start | bytes 18874376 | tf_op jit(solution)/shard_map/ppermute | solution.py:21
  363.9 17.0 %copy-start.1 = (bf16[128,6144]{1,0:T(8,128)(2,1)S(1)}, bf16[128,6144]{1,0:T(8,128)(2,1)}, u32[]{:S(2)}) copy-start(bf16[128,6144]{1,0:T(8,128)(2,1)} %param.5) | copy-start | bytes 4718596
  364.0 96.1 %all-gather.2.cloned.1.call-start = ((), (), s32[]{:S(2)}) async-start(), calls=%async_computation.2 | async-start | bytes 14155776 | tf_op jit(solution)/shard_map/all_gather | solution.py:37
Sparse Core Ops, SparseCore 0:
  364.1 16.8 reduce-scatter.1
  386.0 74.0 all-gather.1
